TPU v7x, 256 devices: a whole 4x4x8 slice. The times are simulated.
256 devices in a mesh: row: 8 (over z), col: 32 (over x, y, core).
Axes of the slice: x: 4, y: 4, z: 8, core: 2. Of those that a mesh axis runs over, the one named last changes fastest.
Arguments:
- tile_data: bfloat16 [8, 32, 32, 256, 256], P('row', 'col'), may hold values from -0.125 to 0.125
- tile_row_block: int32 [8, 32, 32], P('row', 'col'), may hold values from 0 to 63
- tile_column_block: int32 [8, 32, 32], P('row', 'col'), may hold values from 0 to 63
- tile_count: int32 [8, 32], P('row', 'col'), may hold values from 1 to 32, as said below
- saved_primal: float32 [3, 524288], P(None, 'col'), may hold values from 0 to 1
- saved_dual: float32 [3, 131072], P(None, 'row'), may hold values from 0 to 1
- primal_mask: int32 [3, 524288], P(None, 'col'), may hold values 0 or 1
- dual_mask: int32 [3, 131072], P(None, 'row'), may hold values 0 or 1
- cost_vector: float32 [524288], P('col'), may hold values from -6 to 6
- demand: float32 [131072], P('row'), may hold values from -6 to 6
- upper_bound: float32 [524288], P('col'), may hold values from 0.5 to 1.5
- step_sizes: float32 [2], replicated, may hold values from 0.2 to 0.4
- primal_cotangent: float32 [524288], P('col'), may hold values from -6 to 6
- dual_cotangent: float32 [131072], P('row'), may hold values from -6 to 6
Outputs:
- primal_adjoint: float32 [524288], P('col')
- dual_adjoint: float32 [131072], P(('row', 'col'))
- step_gradients: float32 [2], replicated
Inputs may be any that keep to these rules, and one draw needn't show every extreme that they name: `tile_count`: block positions may repeat, and tiles at one position add; slots at and beyond a device's count are ignored. In every index of row some device has 32 live slots.
All inputs are finite; a program needn't handle non-finite values. No bound on the sum of `primal_mask` or of `dual_mask` on one device may be relied on, other than what follows from the above.
Results may differ from a plain program's by a relative error of at most 0.00071.
Values may be sent and summed in bfloat16 or wider, within the bound.
A program may use at most 64 MiB of HBM per device.

v0:
```python
import math
import jax
import jax.numpy as jnp
from jax import lax
from jax.sharding import PartitionSpec as P


def block_terms(tile_part, in_part, out_part, live_part, vectors, out_blocks, transpose):
    tile_width = tile_part.shape[-1]
    blocks = vectors.reshape(vectors.shape[0], -1, tile_width)
    picked = jnp.take(blocks, in_part, axis=1)
    einsum_form = "sij,bsi->bsj" if transpose else "sij,bsj->bsi"
    products = jnp.einsum(einsum_form, tile_part, picked, preferred_element_type=jnp.float32)
    products = products * live_part[None, :, None]
    selector = (out_part[:, None] == jnp.arange(out_blocks, dtype=jnp.int32)[None, :]).astype(
        jnp.float32
    )
    summed = jnp.einsum("sn,bsi->bni", selector, products, precision=lax.Precision.HIGHEST)
    return summed.reshape(vectors.shape[0], out_blocks * tile_width)


def tile_apply(tile_stack, in_index, out_index, live_count, vectors, out_blocks, transpose):
    slot_count = tile_stack.shape[0]
    live_slots = (jnp.arange(slot_count, dtype=jnp.int32) < live_count).astype(jnp.float32)
    return block_terms(tile_stack, in_index, out_index, live_slots, vectors, out_blocks, transpose)


def local(
    tile_data,
    tile_row_block,
    tile_column_block,
    tile_count,
    saved_primal,
    saved_dual,
    primal_mask,
    dual_mask,
    cost_vector,
    demand,
    upper_bound,
    step_sizes,
    primal_cotangent,
    dual_cotangent,
):
    slot_count = tile_data.shape[2]
    tile_width = tile_data.shape[-1]
    tile_stack = tile_data.reshape(slot_count, tile_width, tile_width)
    row_blocks = tile_row_block.reshape(slot_count)
    column_blocks = tile_column_block.reshape(slot_count)
    live_count = tile_count.reshape(())
    iterations = saved_primal.shape[0]
    row_length = saved_dual.shape[1]
    column_length = saved_primal.shape[1]
    share_rows = row_length // lax.axis_size("col")
    share_start = lax.axis_index("col") * share_rows
    column_part = column_length // lax.axis_size("row")
    column_start = lax.axis_index("row") * column_part
    tau = step_sizes[0]
    sigma = step_sizes[1]

    def forward(vectors):
        return tile_apply(
            tile_stack,
            column_blocks,
            row_blocks,
            live_count,
            vectors,
            row_length // tile_width,
            False,
        )

    def backward(vectors):
        return tile_apply(
            tile_stack,
            row_blocks,
            column_blocks,
            live_count,
            vectors,
            column_length // tile_width,
            True,
        )

    def row_share(array):
        return lax.dynamic_slice_in_dim(array, share_start, share_rows, array.ndim - 1)

    def column_share(array):
        return lax.dynamic_slice_in_dim(array, column_start, column_part, array.ndim - 1)

    dual_partial = backward(saved_dual.astype(jnp.bfloat16))
    reduced = cost_vector[None, :] - lax.psum(dual_partial, "row")
    half = jnp.clip(saved_primal - tau * reduced, 0.0, upper_bound[None, :])
    extrapolated = (2.0 * half - saved_primal).astype(jnp.bfloat16)
    masks_x = primal_mask.astype(jnp.float32)
    adjoint_x = primal_cotangent
    partial_value = forward(extrapolated)
    residual_share = row_share(demand[None, :] - lax.psum(partial_value, "col"))
    adjoint_y = dual_cotangent
    masks_y = dual_mask.astype(jnp.float32)
    anchor_x = jnp.zeros_like(adjoint_x)
    anchor_y = jnp.zeros_like(adjoint_y)
    tau_sum = jnp.zeros((), jnp.float32)
    sigma_sum = jnp.zeros((), jnp.float32)
    for step in reversed(range(iterations)):
        weight = (step + 1.0) / (step + 2.0)
        anchor_x = anchor_x + (1.0 - weight) * adjoint_x
        anchor_y = anchor_y + (1.0 - weight) * adjoint_y
        dual_term = masks_y[step] * weight * adjoint_y
        sigma_local = jnp.sum(row_share(dual_term) * residual_share[step])
        spread = dual_term.astype(jnp.bfloat16)
        back_partial = backward(spread[None, :])
        back = lax.psum(back_partial, "row")[0]
        primal_term = masks_x[step] * (weight * adjoint_x - 2.0 * sigma * back)
        tau_local = jnp.sum(-column_share(primal_term) * column_share(reduced[step]))
        primal_input = primal_term.astype(jnp.bfloat16)
        adjoint_x = primal_term + sigma * back
        image = forward(primal_input[None, :])
        image_rows = lax.psum(image, "col")[0]
        adjoint_y = dual_term + tau * image_rows
        tau_total, sigma_total = lax.psum((tau_local, sigma_local), ("row", "col"))
        tau_sum = tau_sum + tau_total
        sigma_sum = sigma_sum + sigma_total
    primal_adjoint = adjoint_x + anchor_x
    dual_adjoint = row_share(adjoint_y + anchor_y)
    total_columns = column_length * lax.axis_size("col")
    total_rows = row_length * lax.axis_size("row")
    gradients = jnp.stack([tau_sum / math.sqrt(total_columns), sigma_sum / math.sqrt(total_rows)])
    return (primal_adjoint, dual_adjoint, gradients)


def solution(mesh):
    placed = (
        P("row", "col", None, None, None),
        P("row", "col", None),
        P("row", "col", None),
        P("row", "col"),
        P(None, "col"),
        P(None, "row"),
        P(None, "col"),
        P(None, "row"),
        P("col"),
        P("row"),
        P("col"),
        P(),
        P("col"),
        P("row"),
    )
    return jax.shard_map(
        local,
        mesh=mesh,
        in_specs=placed,
        out_specs=(P("col"), P(("row", "col")), P()),
        check_vma=False,
    )
```

profile of v0, /device:TPU:1, one launch (start us, length us, event | category | flops | bytes accessed | tf_op | source)
XLA Modules:
  0.0 686.6 jit_solution(12237295428847181642)
XLA Ops:
  8.7 1.0 convert_element_type.25
  12.1 2.8 fusion.14
  17.5 68.9 %all-reduce.10.cloned.1.call-done = f32[1,16384]{1,0:T(1,128)} async-done(((f32[1,16384]{1,0:T(1,128)}), f32[1,16384]{1,0:T(1,128)}) %all-reduce.10.cloned.1.call-update) | async-done | bytes 65552 | tf_op jit(solution)/shard_map/psum | solution.py:110
  86.4 1.6 broadcast_multiply_fusion.5
  88.7 3.4 fusion.12
  93.9 108.8 %all-reduce.12.cloned.1.call-done = f32[1,16384]{1,0:T(1,128)} async-done(((f32[1,16384]{1,0:T(1,128)}), f32[1,16384]{1,0:T(1,128)}) %all-reduce.12.cloned.1.call-update) | async-done | bytes 65552 | tf_op jit(solution)/shard_map/psum | solution.py:116
  202.7 1.5 broadcast_multiply_fusion.2
  204.9 2.8 fusion.10
  208.9 2.9 fusion.2
  211.7 62.4 %all-reduce.14.cloned.1.call-done = f32[1,16384]{1,0:T(1,128)} async-done(((f32[1,16384]{1,0:T(1,128)}), f32[1,16384]{1,0:T(1,128)}) %all-reduce.14.cloned.1.call-update) | async-done | bytes 65552 | tf_op jit(solution)/shard_map/psum | solution.py:110
  274.1 1.6 broadcast_multiply_fusion.4
  276.4 3.4 fusion.8
  282.1 108.3 %all-reduce.16.cloned.1.call-done = f32[1,16384]{1,0:T(1,128)} async-done(((f32[1,16384]{1,0:T(1,128)}), f32[1,16384]{1,0:T(1,128)}) %all-reduce.16.cloned.1.call-update) | async-done | bytes 65552 | tf_op jit(solution)/shard_map/psum | solution.py:116
  390.4 1.5 broadcast_multiply_fusion.1
  392.7 2.8 fusion.6
  397.3 66.3 %all-reduce.20.cloned.1.call-done = (f32[1,16384]{1,0:T(1,128)}, f32[3,16384]{1,0:T(4,128)}) async-done(((f32[1,16384]{1,0:T(1,128)}, f32[3,16384]{1,0:T(4,128)}), (f32[1,16384]{1,0:T(1,128)}, f32[3,16384]{1,0:T(4,128)})) %all-reduce.20.cloned.1.call-update) | async-done | bytes 262160 | tf_op jit(solution)/shard_map/psum | solution.py:110
  463.7 1.8 subtract_convert_fusion
  465.6 1.6 broadcast_multiply_fusion.3
  467.8 3.4 fusion
  473.8 3.4 fusion.4
  481.4 112.0 %all-reduce.18.cloned.1.call-done = (f32[1,16384]{1,0:T(1,128)}, f32[3,16384]{1,0:T(4,128)}) async-done(((f32[1,16384]{1,0:T(1,128)}, f32[3,16384]{1,0:T(4,128)}), (f32[1,16384]{1,0:T(1,128)}, f32[3,16384]{1,0:T(4,128)})) %all-reduce.18.cloned.1.call-update) | async-done | bytes 262160 | tf_op jit(solution)/shard_map/psum | solution.py:116
  595.5 1.5 broadcast_multiply_fusion
  598.3 1.9 multiply_reduce_fusion.3
  601.6 76.4 %all-reduce = (f32[]{:T(128)}, f32[]{:T(128)}) all-reduce(f32[]{:T(128)S(6)} %add.120, f32[]{:T(128)S(6)} %add.118), channel_id=1, replica_groups=mesh['row'=8,'col'=32] {'row','col'}, use_global_device_ids=true, to_apply=%region_15.18 | all-reduce | flops 2 | bytes 16 | tf_op jit(solution)/shard_map/psum | solution.py:118
  (96 shorter events, 23.9 us)
Async XLA Ops:
  7.2 7.8 %copy-start.6 = (s32[1,1,32]{2,1,0:T(1,128)S(1)}, s32[1,1,32]{2,1,0:T(1,128)}, u32[]{:S(2)}) copy-start(s32[1,1,32]{2,1,0:T(1,128)} %param.20) | copy-start | bytes 388
  7.2 8.9 %copy-start.8 = (f32[2]{0:T(128)S(1)}, f32[2]{0:T(128)}, u32[]{:S(2)}) copy-start(f32[2]{0:T(128)} %param.29) | copy-start | bytes 28
  7.2 9.4 %copy-start.1 = (s32[3,16384]{1,0:T(4,128)S(1)}, s32[3,16384]{1,0:T(4,128)}, u32[]{:S(2)}) copy-start(s32[3,16384]{1,0:T(4,128)} %param.24) | copy-start | bytes 589828
  7.2 80.8 %copy-start.3 = (f32[16384]{0:T(1024)S(1)}, f32[16384]{0:T(1024)}, u32[]{:S(2)}) copy-start(f32[16384]{0:T(1024)} %param.30) | copy-start | bytes 196612
  7.2 79.2 %all-reduce.10.cloned.1.call-start = ((), (), s32[]{:S(2)}) async-start(), calls=%async_computation | async-start | bytes 131072 | tf_op jit(solution)/shard_map/psum | solution.py:110
  14.9 77.1 %copy-start.7 = (s32[1,1,32]{2,1,0:T(1,128)S(1)}, s32[1,1,32]{2,1,0:T(1,128)}, u32[]{:S(2)}) copy-start(s32[1,1,32]{2,1,0:T(1,128)} %param.19) | copy-start | bytes 388
  14.9 78.2 %copy-start = (f32[3,16384]{1,0:T(4,128)S(1)}, f32[3,16384]{1,0:T(4,128)}, u32[]{:S(2)}) copy-start(f32[3,16384]{1,0:T(4,128)} %param.23) | copy-start | bytes 589828
  16.0 186.7 %all-reduce.12.cloned.1.call-start = ((), (), s32[]{:S(2)}) async-start(), calls=%async_computation.1 | async-start | bytes 131072 | tf_op jit(solution)/shard_map/psum | solution.py:116
  93.1 181.0 %all-reduce.14.cloned.1.call-start = ((), (), s32[]{:S(2)}) async-start(), calls=%async_computation.2 | async-start | bytes 131072 | tf_op jit(solution)/shard_map/psum | solution.py:110
  208.8 181.6 %all-reduce.16.cloned.1.call-start = ((), (), s32[]{:S(2)}) async-start(), calls=%async_computation.3 | async-start | bytes 131072 | tf_op jit(solution)/shard_map/psum | solution.py:116
  279.8 183.9 %copy-start.2 = (f32[3,16384]{1,0:T(4,128)S(1)}, f32[3,16384]{1,0:T(4,128)}, u32[]{:S(2)}) copy-start(f32[3,16384]{1,0:T(4,128)} %param.22) | copy-start | bytes 589828
  279.8 183.9 %copy-start.4 = (f32[16384]{0:T(1024)S(1)}, f32[16384]{0:T(1024)}, u32[]{:S(2)}) copy-start(f32[16384]{0:T(1024)} %param.28) | copy-start | bytes 196612
  279.8 183.9 %copy-start.5 = (f32[16384]{0:T(1024)S(1)}, f32[16384]{0:T(1024)}, u32[]{:S(2)}) copy-start(f32[16384]{0:T(1024)} %param.26) | copy-start | bytes 196612
  280.8 182.9 %all-reduce.20.cloned.1.call-start = ((), (), s32[]{:S(2)}) async-start(), calls=%async_computation.5 | async-start | bytes 655360 | tf_op jit(solution)/shard_map/psum | solution.py:110
  396.5 196.9 %all-reduce.18.cloned.1.call-start = ((), (), s32[]{:S(2)}) async-start(), calls=%async_computation.4 | async-start | bytes 655360 | tf_op jit(solution)/shard_map/psum | solution.py:116
Sparse Core Ops, SparseCore 0:
  16.1 70.2 all-reduce.9
  93.3 109.3 all-reduce.11
  208.9 65.1 all-reduce.13
  280.9 109.3 all-reduce.15
  396.6 66.9 all-reduce.19
  478.4 115.0 all-reduce.17
where the time goes:
time: 688 us; the launch traced here: 687 us
  waiting for transfers between devices  527 us (77%)
  blocking collectives  76.4 us (11%)
  matrix products  27.4 us (4%)
  other arithmetic  22.2 us (3%)
  between operations  20.9 us (3%)
  local copies, waits for them, and re-layouts  12.7 us (2%)
    psum x3, waiting for transfers between devices, local(): image_rows = lax.psum(image, 'col')[0]  329 us
    psum x3, waiting for transfers between devices, local(): back = lax.psum(back_partial, 'row')[0]  198 us
    psum x1, blocking collectives, local(): tau_total, sigma_total = lax.psum((tau_local, sigma_local), ('row', 'col'))  76.4 us
    dot_general x8, matrix products, block_terms(): jnp.einsum(einsum_form, tile_part, picked, preferred_element_type=jnp.flo...  24.8 us
  transfers between devices with their start and end apart: 6, of which 6 were waited for; matrix products, arithmetic and copies ran while one was open for 1% of the time, Pallas kernels for 0%

commit v1 on v0

--- a/solution.py
+++ b/solution.py
@@ -3,6 +3,11 @@
 import jax.numpy as jnp
 from jax import lax
 from jax.sharding import PartitionSpec as P
+
+
+def add_all(array, axis):
+    pieces = lax.all_gather(array, axis)
+    return jnp.sum(pieces, axis=0)
 
 
 def block_terms(tile_part, in_part, out_part, live_part, vectors, out_blocks, transpose):
@@ -107,7 +112,7 @@
         sigma_local = jnp.sum(row_share(dual_term) * residual_share[step])
         spread = dual_term.astype(jnp.bfloat16)
         back_partial = backward(spread[None, :])
-        back = lax.psum(back_partial, "row")[0]
+        back = add_all(back_partial, "row")[0]
         primal_term = masks_x[step] * (weight * adjoint_x - 2.0 * sigma * back)
         tau_local = jnp.sum(-column_share(primal_term) * column_share(reduced[step]))
         primal_input = primal_term.astype(jnp.bfloat16)

time: 688 us -> 586 us (0.85)
  waiting for transfers between devices: 527 us -> 363 us
  blocking collectives: 76.4 us -> 142 us
    psum x3 -> x1, waiting for transfers between devices: 198 us -> 36 us  [local(): reduced = cost_vector[None, :] - lax.psum(dual_partial, 'row')]
    all_gather x0 -> x3, blocking collectives: none -> 66.1 us  [add_all(): pieces = lax.all_gather(array, axis)]
  transfers between devices with their start and end apart: 6 -> 4, of which waited for: 6 -> 4; matrix products, arithmetic and copies ran while one was open for 1% -> 3% of each run, Pallas kernels for 0% -> 0%
where the time goes in v1:
time: 586 us; the launch traced here: 585 us
  waiting for transfers between devices  363 us (62%)
  blocking collectives  142 us (24%)
  matrix products  27.4 us (5%)
  other arithmetic  20.5 us (3%)
  between operations  20.5 us (3%)
  local copies, waits for them, and re-layouts  10.8 us (2%)
    psum x3, waiting for transfers between devices, local(): image_rows = lax.psum(image, 'col')[0]  327 us
    psum x1, blocking collectives, local(): tau_total, sigma_total = lax.psum((tau_local, sigma_local), ('row', 'col'))  76.4 us
    all_gather x3, blocking collectives, add_all(): pieces = lax.all_gather(array, axis)  66.1 us
    psum x1, waiting for transfers between devices, local(): reduced = cost_vector[None, :] - lax.psum(dual_partial, 'row')  36 us
    dot_general x8, matrix products, block_terms(): jnp.einsum(einsum_form, tile_part, picked, preferred_element_type=jnp.flo...  24.9 us
  transfers between devices with their start and end apart: 4, of which 4 were waited for; matrix products, arithmetic and copies ran while one was open for 3% of the time, Pallas kernels for 0%

profile of v1, /device:TPU:1, one launch (start us, length us, event | category | flops | bytes accessed | tf_op | source)
XLA Modules:
  0.0 585.1 jit_solution(1149535442940587989)
XLA Ops:
  9.9 1.0 convert_element_type.25
  11.1 0.9 fusion.84
  13.4 2.8 fusion.14
  16.6 23.7 %all_gather.9 = f32[8,1,16384]{2,1,0:T(1,128)S(1)} all-gather(f32[1,1,16384]{2,1,0:T(1,128)S(1)} %all_gather_reshape.9), channel_id=1, replica_groups=mesh['row'=8,'col'=32] {'row'}, dimensions={0}, use_global_device_ids=true | all-gather | bytes 589824 | tf_op jit(solution)/shard_map/all_gather | solution.py:9
  42.9 3.4 fusion.12
  48.0 2.9 fusion.19
  50.9 107.9 %all-reduce.7.cloned.1.call-done = f32[1,16384]{1,0:T(1,128)} async-done(((f32[1,16384]{1,0:T(1,128)}), f32[1,16384]{1,0:T(1,128)}) %all-reduce.7.cloned.1.call-update) | async-done | bytes 65552 | tf_op jit(solution)/shard_map/psum | solution.py:121
  158.8 1.5 broadcast_multiply_fusion.2
  161.1 2.8 fusion.10
  164.3 20.9 %all_gather.10 = f32[8,1,16384]{2,1,0:T(1,128)S(1)} all-gather(f32[1,1,16384]{2,1,0:T(1,128)S(1)} %all_gather_reshape.10), channel_id=1, replica_groups=mesh['row'=8,'col'=32] {'row'}, dimensions={0}, use_global_device_ids=true | all-gather | bytes 589824 | tf_op jit(solution)/shard_map/all_gather | solution.py:9
  187.0 3.4 fusion.8
  193.5 107.4 %all-reduce.9.cloned.1.call-done = f32[1,16384]{1,0:T(1,128)} async-done(((f32[1,16384]{1,0:T(1,128)}), f32[1,16384]{1,0:T(1,128)}) %all-reduce.9.cloned.1.call-update) | async-done | bytes 65552 | tf_op jit(solution)/shard_map/psum | solution.py:121
  300.9 1.5 broadcast_multiply_fusion.1
  303.1 2.8 fusion.6
  306.4 21.4 %all_gather.11 = f32[8,1,16384]{2,1,0:T(1,128)S(1)} all-gather(f32[1,1,16384]{2,1,0:T(1,128)S(1)} %all_gather_reshape.11), channel_id=1, replica_groups=mesh['row'=8,'col'=32] {'row'}, dimensions={0}, use_global_device_ids=true | all-gather | bytes 589824 | tf_op jit(solution)/shard_map/all_gather | solution.py:9
  329.5 3.4 fusion.4
  333.9 36.0 %all-reduce.11.cloned.1.call-done = f32[3,16384]{1,0:T(4,128)} async-done(((f32[3,16384]{1,0:T(4,128)}), f32[3,16384]{1,0:T(4,128)}) %all-reduce.11.cloned.1.call-update) | async-done | bytes 196624 | tf_op jit(solution)/shard_map/psum | solution.py:94
  369.9 1.8 subtract_convert_fusion
  372.5 3.4 fusion.25
  380.4 111.8 %all-reduce.13.cloned.1.call-done = (f32[1,16384]{1,0:T(1,128)}, f32[3,16384]{1,0:T(4,128)}) async-done(((f32[1,16384]{1,0:T(1,128)}, f32[3,16384]{1,0:T(4,128)}), (f32[1,16384]{1,0:T(1,128)}, f32[3,16384]{1,0:T(4,128)})) %all-reduce.13.cloned.1.call-update) | async-done | bytes 262160 | tf_op jit(solution)/shard_map/psum | solution.py:121
  493.7 1.5 broadcast_multiply_fusion
  495.2 2.0 multiply_reduce_fusion.3
  499.2 1.2 add_add_fusion
  500.4 76.4 %all-reduce = (f32[]{:T(128)}, f32[]{:T(128)}) all-reduce(f32[]{:T(128)S(6)} %add.114, f32[]{:T(128)S(6)} %add.112), channel_id=1, replica_groups=mesh['row'=8,'col'=32] {'row','col'}, use_global_device_ids=true, to_apply=%region_15.18 | all-reduce | flops 2 | bytes 16 | tf_op jit(solution)/shard_map/psum | solution.py:123
  (93 shorter events, 22.7 us)
Async XLA Ops:
  7.2 9.1 %copy-start.7 = (s32[1,1,32]{2,1,0:T(1,128)S(1)}, s32[1,1,32]{2,1,0:T(1,128)}, u32[]{:S(2)}) copy-start(s32[1,1,32]{2,1,0:T(1,128)} %param.20) | copy-start | bytes 388
  7.2 33.2 %copy-start.6 = (f32[2]{0:T(128)S(1)}, f32[2]{0:T(128)}, u32[]{:S(2)}) copy-start(f32[2]{0:T(128)} %param.29) | copy-start | bytes 28
  7.2 33.8 %copy-start.1 = (s32[3,16384]{1,0:T(4,128)S(1)}, s32[3,16384]{1,0:T(4,128)}, u32[]{:S(2)}) copy-start(s32[3,16384]{1,0:T(4,128)} %param.24) | copy-start | bytes 589828
  7.2 34.9 %copy-start.2 = (f32[16384]{0:T(1024)S(1)}, f32[16384]{0:T(1024)}, u32[]{:S(2)}) copy-start(f32[16384]{0:T(1024)} %param.30) | copy-start | bytes 196612
  7.2 151.6 %all-reduce.7.cloned.1.call-start = ((), (), s32[]{:S(2)}) async-start(), calls=%async_computation | async-start | bytes 131072 | tf_op jit(solution)/shard_map/psum | solution.py:121
  16.2 30.0 %copy-start.8 = (s32[1,1,32]{2,1,0:T(1,128)S(1)}, s32[1,1,32]{2,1,0:T(1,128)}, u32[]{:S(2)}) copy-start(s32[1,1,32]{2,1,0:T(1,128)} %param.19) | copy-start | bytes 388
  16.2 31.1 %copy-start = (f32[3,16384]{1,0:T(4,128)S(1)}, f32[3,16384]{1,0:T(4,128)}, u32[]{:S(2)}) copy-start(f32[3,16384]{1,0:T(4,128)} %param.23) | copy-start | bytes 589828
  47.3 253.6 %all-reduce.9.cloned.1.call-start = ((), (), s32[]{:S(2)}) async-start(), calls=%async_computation.1 | async-start | bytes 131072 | tf_op jit(solution)/shard_map/psum | solution.py:121
  191.4 178.5 %all-reduce.11.cloned.1.call-start = ((), (), s32[]{:S(2)}) async-start(), calls=%async_computation.2 | async-start | bytes 524288 | tf_op jit(solution)/shard_map/psum | solution.py:94
  192.6 299.6 %all-reduce.13.cloned.1.call-start = ((), (), s32[]{:S(2)}) async-start(), calls=%async_computation.3 | async-start | bytes 655360 | tf_op jit(solution)/shard_map/psum | solution.py:121
  306.0 63.9 %copy-start.3 = (f32[3,16384]{1,0:T(4,128)S(1)}, f32[3,16384]{1,0:T(4,128)}, u32[]{:S(2)}) copy-start(f32[3,16384]{1,0:T(4,128)} %param.22) | copy-start | bytes 589828
  306.0 63.9 %copy-start.4 = (f32[16384]{0:T(1024)S(1)}, f32[16384]{0:T(1024)}, u32[]{:S(2)}) copy-start(f32[16384]{0:T(1024)} %param.28) | copy-start | bytes 196612
  306.0 63.9 %copy-start.5 = (f32[16384]{0:T(1024)S(1)}, f32[16384]{0:T(1024)}, u32[]{:S(2)}) copy-start(f32[16384]{0:T(1024)} %param.26) | copy-start | bytes 196612
Sparse Core Ops, SparseCore 0:
  47.4 111.3 all-reduce.6
  191.5 109.3 all-reduce.8
  303.2 66.6 all-reduce.10
  377.2 114.9 all-reduce.12
